TPU v7x, 256 devices: a whole 4x4x8 slice. The times are simulated.
256 devices in a mesh: dp: 8 (over z), seq: 32 (over y, x, core).
Axes of the slice: x: 4, y: 4, z: 8, core: 2. Of those that a mesh axis runs over, the one named last changes fastest.
Arguments:
- embeddings: bfloat16 [8, 16384, 512], P('dp', 'seq'), may hold values from -6 to 6
- user_ids: int32 [8, 16384], P('dp', 'seq'), may hold values from 0 to 63, never falling along the last dimension, each value on 1 to 512 neighbouring positions
- time_gaps: int32 [8, 16384], P('dp', 'seq'), may hold values from 0 to 16
- proj_weight: bfloat16 [512, 2048], replicated, may hold values from -0.25 to 0.25
- out_weight: bfloat16 [512, 512], replicated, may hold values from -0.25 to 0.25
- frequencies: float32 [64], replicated, may hold values from 0.001 to 0.1
- time_mix: float32 [4, 64], replicated, may hold values from -0.9 to 0.9
- cotangent: bfloat16 [8, 16384, 512], P('dp', 'seq'), may hold values from -6 to 6
Outputs:
- layer_out: bfloat16 [8, 16384, 512], P('dp', 'seq')
- grad_input: bfloat16 [8, 16384, 512], P('dp', 'seq')
- grad_proj: float32 [512, 2048], P('seq')
- grad_out_weight: float32 [512, 512], P('seq')
- grad_time_mix: float32 [4, 64], replicated
Inputs may be any that keep to these rules, and one draw needn't show every extreme that they name: `user_ids`: within a stream the ids never fall, so each user's events are consecutive; a user holds at most 512 events, and some user holds exactly that many.
All inputs are finite; a program needn't handle non-finite values.
Results may differ from a plain program's by a relative error of at most 0.019.
Values may be sent and summed in bfloat16 or wider, within the bound.
A program may use at most 64 MiB of HBM per device.

v0:
```python
import jax
import jax.numpy as jnp
from jax import lax
from jax.sharding import PartitionSpec as P

BLOCK = 512
REACH = 1
EPSILON = 1e-05
HIGH = lax.Precision.HIGHEST


def entering(value, axis, join, neutral):
    count, mine = (lax.axis_size(axis), lax.axis_index(axis))
    pieces = jax.tree.map(lambda part: lax.all_gather(part, axis), value)
    total = jax.tree.map(
        lambda part, zero: jnp.full_like(part, 0) + jnp.asarray(zero, part.dtype), value, neutral
    )

    def turn(position, total):
        longer = join(total, jax.tree.map(lambda part: part[position], pieces))
        return jax.tree.map(lambda new, old: jnp.where(position < mine, new, old), longer, total)

    return lax.fori_loop(0, count - 1, turn, total)


def shifted(array, axis, by):
    length = lax.axis_size(axis)
    pairs = [(i, i + by) for i in range(length) if 0 <= i + by < length]
    return lax.ppermute(array, axis, pairs)


def silu_slope(value):
    sigma = jax.nn.sigmoid(value)
    return sigma * (1.0 + value * (1.0 - sigma))


def run_times(users, gaps):
    count = users.shape[0]
    running = jnp.cumsum(gaps)
    position = jnp.arange(count, dtype=jnp.int32)
    before = jnp.concatenate([users[:1] - 1, users[:-1]])
    opening = jnp.where(users != before, position, 0)
    first = lax.cummax(opening, axis=0)
    return running - (running[first] - gaps[first])


def combine(earlier, later):
    valid_a, user_a, total_a, whole_a = earlier
    valid_b, user_b, total_b, whole_b = later
    both = (valid_a == 1) & (valid_b == 1)
    has_later = valid_b == 1
    same = user_a == user_b
    joined = jnp.where((whole_b == 1) & same, total_a + total_b, total_b)
    merged_whole = jnp.where((whole_a == 1) & (whole_b == 1) & same, 1, 0)
    return (
        jnp.maximum(valid_a, valid_b).astype(jnp.int32),
        jnp.where(has_later, user_b, user_a).astype(jnp.int32),
        jnp.where(both, joined, jnp.where(has_later, total_b, total_a)).astype(jnp.int32),
        jnp.where(both, merged_whole, jnp.where(has_later, whole_b, whole_a)).astype(jnp.int32),
    )


def time_features(times, frequencies, time_mix):
    angles = times.astype(jnp.float32)[:, None] * frequencies[None, :]
    cosines = jnp.cos(angles)
    sines = jnp.sin(angles)
    key_time = jnp.concatenate([cosines, sines], 1).astype(jnp.bfloat16)
    query_time = jnp.concatenate(
        [cosines[:, None, :] * time_mix[None], sines[:, None, :] * time_mix[None]], 2
    ).astype(jnp.bfloat16)
    return (cosines, sines, key_time, query_time)


def project(events, proj_weight):
    values_wide = events.astype(jnp.float32)
    scale_in = lax.rsqrt(jnp.mean(values_wide * values_wide, -1, keepdims=True) + EPSILON)
    unit_rows = values_wide * scale_in
    normed = unit_rows.astype(jnp.bfloat16)
    preact = jnp.dot(normed, proj_weight, preferred_element_type=jnp.float32)
    hidden = jax.nn.silu(preact).astype(jnp.bfloat16)
    return (scale_in, unit_rows, normed, preact, hidden)


def pair_scores(query, query_time, keys, key_time):
    inverse = query.shape[-1] ** (-0.5)
    return jnp.einsum(
        "qhd,khd->hqk", query, keys, preferred_element_type=jnp.float32
    ) * inverse + jnp.einsum(
        "qhf,kf->hqk", query_time, key_time, preferred_element_type=jnp.float32
    )


def pair_mask(query_user, query_pos, key_user, key_pos):
    return (
        (key_user[None, :] == query_user[:, None])
        & (key_pos[None, :] <= query_pos[:, None])
        & (key_pos[None, :] >= 0)
    )


def forward_pair(operands):
    query, query_time, query_user, query_pos, keys, values, key_time, key_user, key_pos = operands
    mask = pair_mask(query_user, query_pos, key_user, key_pos)
    scores = pair_scores(query, query_time, keys, key_time)
    weights = jnp.where(mask[None], jax.nn.silu(scores), 0.0).astype(jnp.bfloat16)
    return jnp.einsum("hqk,khd->qhd", weights, values, preferred_element_type=jnp.float32)


def forward_none(operands):
    return jnp.zeros(operands[0].shape, jnp.float32)


def backward_pair(operands):
    (
        query,
        query_time,
        query_user,
        query_pos,
        grad_tile,
        keys,
        values,
        key_time,
        key_user,
        key_pos,
    ) = operands
    inverse = query.shape[-1] ** (-0.5)
    mask = pair_mask(query_user, query_pos, key_user, key_pos)
    scores = pair_scores(query, query_time, keys, key_time)
    weights = jnp.where(mask[None], jax.nn.silu(scores), 0.0).astype(jnp.bfloat16)
    grad_weights = jnp.einsum("qhd,khd->hqk", grad_tile, values, preferred_element_type=jnp.float32)
    grad_scores = jnp.where(mask[None], grad_weights * silu_slope(scores), 0.0).astype(jnp.bfloat16)
    value_part = jnp.einsum("hqk,qhd->khd", weights, grad_tile, preferred_element_type=jnp.float32)
    key_part = (
        jnp.einsum("hqk,qhd->khd", grad_scores, query, preferred_element_type=jnp.float32) * inverse
    )
    query_part = (
        jnp.einsum("hqk,khd->qhd", grad_scores, keys, preferred_element_type=jnp.float32) * inverse
    )
    qtime_part = jnp.einsum(
        "hqk,kf->qhf", grad_scores, key_time, preferred_element_type=jnp.float32
    )
    return (query_part, qtime_part, key_part, value_part)


def backward_none(operands):
    return (
        jnp.zeros(operands[0].shape, jnp.float32),
        jnp.zeros(operands[1].shape, jnp.float32),
        jnp.zeros(operands[5].shape, jnp.float32),
        jnp.zeros(operands[6].shape, jnp.float32),
    )


def body(
    embeddings, user_ids, time_gaps, proj_weight, out_weight, frequencies, time_mix, cotangent
):
    events = embeddings[0]
    users = user_ids[0]
    gaps = time_gaps[0]
    upstream = cotangent[0]
    count = events.shape[0]
    model_width = events.shape[1]
    heads = time_mix.shape[0]
    head_size = model_width // heads
    freq_count = frequencies.shape[0]
    device = lax.axis_index("seq")
    seq_devices = lax.axis_size("seq")
    local_times = run_times(users, gaps)
    summary = (
        jnp.ones((1,), jnp.int32),
        users[-1:],
        local_times[-1:],
        (users[:1] == users[-1:]).astype(jnp.int32),
    )
    identity = (
        jnp.zeros((1,), jnp.int32),
        jnp.zeros((1,), jnp.int32),
        jnp.zeros((1,), jnp.int32),
        jnp.zeros((1,), jnp.int32),
    )
    carried = entering(summary, "seq", combine, identity)
    times = (
        local_times + jnp.where((carried[0] == 1) & (users == carried[1]), carried[2], 0)
    ).astype(jnp.int32)
    cosines, sines, key_time, query_time = time_features(times, frequencies, time_mix)
    scale_in, unit_rows, normed, preact, hidden = project(events, proj_weight)
    gate_part = hidden[:, :model_width]
    value_flat = hidden[:, model_width : 2 * model_width]
    query_flat = hidden[:, 2 * model_width : 3 * model_width]
    key_flat = hidden[:, 3 * model_width :]
    user_marks = users.astype(jnp.bfloat16)
    positions = device * count + jnp.arange(count, dtype=jnp.int32)
    sources = []
    distance = 1
    received = shifted((key_flat, value_flat, key_time, user_marks), "seq", distance)
    sources.append(
        (received[0], received[1], received[2], received[3], positions - distance * count)
    )
    sources.append((key_flat, value_flat, key_time, user_marks, positions))

    def head_tile(flat):
        return flat.reshape(BLOCK, heads, head_size)

    def key_operands(source_index):
        keys, values, times_part, marks, places = sources[source_index]
        return (head_tile(keys), head_tile(values), times_part, marks, places)

    def query_operands():
        return (head_tile(query_flat), query_time, user_marks, positions)

    def candidates():
        listed = []
        tile_index = 0
        listed.append((0, tile_index))
        tile_index = 0
        listed.append((REACH, tile_index))
        return listed

    def is_live(query_part, key_part):
        return (key_part[3][-1] >= query_part[2][0]) & (key_part[4][-1] >= 0)

    query_part = query_operands()
    total = jnp.zeros((BLOCK, heads, head_size), jnp.float32)
    for pair in candidates():
        key_part = key_operands(pair[0])
        total = total + lax.cond(
            is_live(query_part, key_part), forward_pair, forward_none, query_part + key_part
        )
    attended = total.reshape(count, model_width)
    scale_mid = lax.rsqrt(jnp.mean(attended * attended, -1, keepdims=True) + EPSILON)
    normed_mid = attended * scale_mid
    gate_wide = gate_part.astype(jnp.float32)
    gated = (normed_mid * gate_wide).astype(jnp.bfloat16)
    layer_out = (
        events.astype(jnp.float32) + jnp.dot(gated, out_weight, preferred_element_type=jnp.float32)
    ).astype(jnp.bfloat16)
    grad_gated = jnp.einsum("ef,df->ed", upstream, out_weight, preferred_element_type=jnp.float32)
    grad_gate = grad_gated * normed_mid
    grad_mid = grad_gated * gate_wide
    grad_attended = (
        scale_mid * (grad_mid - normed_mid * jnp.mean(grad_mid * normed_mid, -1, keepdims=True))
    ).astype(jnp.bfloat16)
    key_grads = {}
    query_part = query_operands()
    grad_tile = head_tile(grad_attended)
    grad_query = jnp.zeros((BLOCK, heads, head_size), jnp.float32)
    grad_qtime = jnp.zeros((BLOCK, heads, 2 * freq_count), jnp.float32)
    for pair in candidates():
        key_part = key_operands(pair[0])
        result = lax.cond(
            is_live(query_part, key_part),
            backward_pair,
            backward_none,
            query_part + (grad_tile,) + key_part,
        )
        grad_query = grad_query + result[0]
        grad_qtime = grad_qtime + result[1]
        key_grads[pair] = (result[2], result[3])

    def source_grads(source_index):
        keys_part = key_grads[source_index, 0][0]
        values_part = key_grads[source_index, 0][1]
        return (keys_part.reshape(count, model_width), values_part.reshape(count, model_width))

    grad_keys_flat, grad_values_flat = source_grads(REACH)
    distance = 1
    partial_keys, partial_values = source_grads(distance - 1)
    returned = (
        shifted(partial_keys.astype(jnp.bfloat16), "seq", -distance).astype(partial_keys.dtype),
        shifted(partial_values.astype(jnp.bfloat16), "seq", -distance).astype(partial_values.dtype),
    )
    grad_keys_flat = grad_keys_flat + returned[0]
    grad_values_flat = grad_values_flat + returned[1]
    grad_query_flat = grad_query.reshape(count, model_width)
    grad_act = jnp.concatenate([grad_gate, grad_values_flat, grad_query_flat, grad_keys_flat], 1)
    grad_pre = (grad_act * silu_slope(preact)).astype(jnp.bfloat16)
    grad_normed = jnp.einsum("ef,df->ed", grad_pre, proj_weight, preferred_element_type=jnp.float32)
    grad_input = (
        upstream.astype(jnp.float32)
        + scale_in
        * (grad_normed - unit_rows * jnp.mean(grad_normed * unit_rows, -1, keepdims=True))
    ).astype(jnp.bfloat16)
    proj_part = jnp.einsum("ed,ef->df", normed, grad_pre, preferred_element_type=jnp.float32)
    out_part = jnp.einsum("ed,ef->df", gated, upstream, preferred_element_type=jnp.float32)
    whole = lax.psum(jnp.concatenate([proj_part, out_part], 1).astype(jnp.bfloat16), "dp")
    shard = lax.psum_scatter(whole, "seq", scatter_dimension=0, tiled=True).astype(jnp.float32)
    grad_mix = jnp.einsum(
        "ehf,ef->hf", grad_qtime[:, :, :freq_count], cosines, precision=HIGH
    ) + jnp.einsum("ehf,ef->hf", grad_qtime[:, :, freq_count:], sines, precision=HIGH)
    grad_mix = lax.psum(grad_mix, ("dp", "seq"))
    factor = float(lax.axis_size("dp") * seq_devices * count) ** (-0.5)
    grad_proj = shard[:, : 4 * model_width] * factor
    grad_out_weight = shard[:, 4 * model_width :] * factor
    return (layer_out[None], grad_input[None], grad_proj, grad_out_weight, grad_mix * factor)


def solution(mesh):
    return jax.shard_map(
        body,
        mesh=mesh,
        in_specs=(
            P("dp", "seq", None),
            P("dp", "seq"),
            P("dp", "seq"),
            P(),
            P(),
            P(),
            P(),
            P("dp", "seq", None),
        ),
        out_specs=(P("dp", "seq", None), P("dp", "seq", None), P("seq", None), P("seq", None), P()),
        check_vma=False,
    )
```

profile of v0, /device:TPU:32, one launch (start us, length us, event | category | flops | bytes accessed | tf_op | source)
XLA Modules:
  0.0 555.3 jit_solution(1448338192975510792)
XLA Ops:
  8.1 2.3 collective-permute-start
  16.4 3.6 gather_fusion.1
  20.0 3.5 gather_fusion
  27.7 16.6 %all-reduce.4 = (s32[32]{0:T(128)S(1)}, s32[32]{0:T(128)S(1)}, s32[32]{0:T(128)S(1)}, s32[32]{0:T(128)S(1)}) all-reduce(s32[32]{0:T(128)S(1)} %dynamic-update-slice, s32[32]{0:T(128)S(1)} %bitcast_dynamic-update-slice_fusion.1, s32[32]{0:T(128)S(1)} %bitcast_dynamic-update-slice_fusion, ...), channel_id=1, replica_groups=mesh['dp'=8,'seq'=32] {'seq'}, use_global_device_ids=true, to_apply=%add | all-reduce | flops 128 | bytes 1024
  44.3 217.0 %while.17 = (s32[]{:T(128)}, s32[1]{0:T(128)}, s32[1]{0:T(128)}, s32[1]{0:T(128)}, s32[]{:T(128)}, /*index=5*/s32[32,1]{0,1:T(1,128)S(1)}, s32[32,1]{0,1:T(1,128...) while((s32[]{:T(128)}, s32[1]{0:T(128)}, s32[1]{0:T(128)}, s32[1]{0:T(128)}, ...), condition=%wide.region_6.7_spmd, body=%wide.region_5.6_spmd.sunk | while | flops 18 | bytes 315 | solution.py:23
  265.4 3.6 multiply_convert_fusion
  271.6 3.8 collective-permute-start.3
  288.4 10.0 %conditional.5 = (f32[512,4,128]{2,0,1:T(8,128)}) conditional(s32[]{:T(128)} %bitcast.54, () %tuple.57, (bf16[512]{0:T(512)(128)(2,1)S(1)}, s32[512]{0:T(512)S(1)}, bf16[512,4,128]{2,1,0:T(4,128)(2,1)S(1)}, bf16[512,4,128]{2,1,0:T(4,128)(2,1)}, bf16[512,128]{1,0:T(8,128)(2,1)S(1)}, /*index=5*/bf16[512,4,128]{2,0,1:T(8,128)(2,1)S(1)}, ...), branch_computations={%region_9.10_spmd, %region_10.11_spmd} | conditional | flops 815268352 | bytes 12195848 | solution.py:226
  289.5 3.7 fusion.14
  293.2 5.2 fusion.12
  309.7 2.8 multiply_convert_fusion.1
  319.1 29.8 %conditional.6 = (f32[512,4,128]{2,0,1:T(8,128)}, f32[512,4,128]{2,0,1:T(8,128)}, f32[512,512]{1,0:T(8,128)}, f32[512,512]{1,0:T(8,128)}) conditional(s32[]{:T(128)} %bitcast.54, () %tuple.59, (bf16[512]{0:T(512)(128)(2,1)S(1)}, s32[512]{0:T(512)S(1)}, bf16[512,4,128]{2,1,0:T(4,128)(2,1)}, bf16[512,4,128]{2,1,0:T(4,128)(2,1)}, ...), branch_computations={%region_13.14_spmd, %region_14.15_spmd} | conditional | flops 1900020224 | bytes 65018056 | solution.py:250
  325.9 2.3 fusion.22
  328.3 4.3 select_convert_fusion.3
  332.6 2.5 copy.107
  335.1 3.6 fusion.23
  338.7 2.5 copy.53
  341.2 2.6 copy.109
  343.8 3.4 fusion.24
  364.6 101.5 %psum.15 = f32[4,64]{1,0:T(4,128)S(1)} all-reduce(f32[4,64]{1,0:T(4,128)S(1)} %add_bitcast_fusion.3), channel_id=1, replica_groups=mesh['dp'=8,'seq'=32] {'dp','seq'}, use_global_device_ids=true, to_apply=%region_20.21 | all-reduce | flops 256 | bytes 2048 | tf_op jit(solution)/shard_map/psum | solution.py:290
  466.1 2.3 fusion.54
  469.0 3.9 fusion.56
  473.0 2.3 fusion.67
  475.3 71.0 %all-reduce.7.cloned.1.call-done = bf16[16,2560]{1,0:T(8,128)(2,1)} async-done(((bf16[16,2560]{1,0:T(8,128)(2,1)}), bf16[16,2560]{1,0:T(8,128)(2,1)}) %all-reduce.7.cloned.1.call-update) | async-done | bytes 81936 | tf_op jit(solution)/shard_map/psum | solution.py:285
  (232 shorter events, 131.3 us)
Async XLA Ops:
  7.2 258.2 %copy-start = (bf16[512,2048]{1,0:T(8,128)(2,1)S(1)}, bf16[512,2048]{1,0:T(8,128)(2,1)}, u32[]{:S(2)}) copy-start(bf16[512,2048]{1,0:T(8,128)(2,1)} %param.21) | copy-start | bytes 6291460
  7.2 16.4 %copy-start.23 = (u32[256]{0:T(256)S(1)}, u32[256]{0:T(256)}, u32[]{:S(2)}) copy-start(u32[256]{0:T(256)} %constant.130) | copy-start | bytes 3076
  7.2 254.1 %copy-start.20 = (s32[1,512]{1,0:T(1,128)S(1)}, s32[1,512]{1,0:T(1,128)}, u32[]{:S(2)}) copy-start(s32[1,512]{1,0:T(1,128)} %param.19) | copy-start | bytes 6148
  7.2 254.1 %copy-start.22 = (f32[64]{0:T(128)S(1)}, f32[64]{0:T(128)}, u32[]{:S(2)}) copy-start(f32[64]{0:T(128)} %param.23) | copy-start | bytes 772
  7.2 258.0 %copy-start.5 = (bf16[1,512,512]{2,1,0:T(8,128)(2,1)S(1)}, bf16[1,512,512]{2,1,0:T(8,128)(2,1)}, u32[]{:S(2)}) copy-start(bf16[1,512,512]{2,1,0:T(8,128)(2,1)} %param.18) | copy-start | bytes 1572868
  7.2 465.7 %reduce-scatter.2.cloned.1.call-start = ((), (), s32[]{:S(2)}) async-start(), calls=%async_computation.1 | async-start | bytes 2703360 | tf_op jit(solution)/shard_map/reduce_scatter | solution.py:286
  8.1 290.3 %collective-permute-start = (bf16[512]{0:T(512)(128)(2,1)S(1)}, bf16[512]{0:T(512)(128)(2,1)}, u32[]{:S(2)}, u32[]{:S(2)}) collective-permute-start(bf16[512]{0:T(512)(128)(2,1)S(1)} %convert_reduce_fusion), channel_id=1, source_target_pairs={{0,1},{1,2},{2,3},{3,4},{4,5},{5,6},{6,7},{7,8},{8,9},{9,10},{10,1... | collective-permute-start | bytes 3080 | tf_op jit(solution)/shard_map/ppermute | solution.py:29
  263.3 41.7 %collective-permute-start.2 = (bf16[512,128]{1,0:T(8,128)(2,1)S(1)}, bf16[512,128]{1,0:T(8,128)(2,1)}, u32[]{:S(2)}, u32[]{:S(2)}) collective-permute-start(bf16[512,128]{1,0:T(8,128)(2,1)S(1)} %pad_maximum_fusion.2), channel_id=1, source_target_pairs={{0,1},{1,2},{2,3},{3,4},{4,5},{5,6},{6,7},{7,8},{8,9},{9,10},{10,1... | collective-permute-start | bytes 393224 | tf_op jit(solution)/shard_map/ppermute | solution.py:29
  265.4 12.1 %copy-start.21 = (f32[4,64]{1,0:T(4,128)S(1)}, f32[4,64]{1,0:T(4,128)}, u32[]{:S(2)}) copy-start(f32[4,64]{1,0:T(4,128)} %param.24) | copy-start | bytes 3076
  271.6 29.4 %collective-permute-start.3 = (bf16[512,512]{1,0:T(8,128)(2,1)}, bf16[512,512]{1,0:T(8,128)(2,1)}, u32[]{:S(2)}, u32[]{:S(2)}) collective-permute-start(bf16[512,512]{1,0:T(8,128)(2,1)} %get-tuple-element.395), channel_id=1, source_target_pairs={{0,1},{1,2},{2,3},{3,4},{4,5},{5,6},{6,7},{7,8},{8,9},{9,10},{10,1... | collective-permute-start | bytes 1572872 | tf_op jit(solution)/shard_map/ppermute | solution.py:29
  275.4 27.6 %collective-permute-start.1 = (bf16[512,512]{1,0:T(8,128)(2,1)}, bf16[512,512]{1,0:T(8,128)(2,1)}, u32[]{:S(2)}, u32[]{:S(2)}) collective-permute-start(bf16[512,512]{1,0:T(8,128)(2,1)} %get-tuple-element.396), channel_id=1, source_target_pairs={{0,1},{1,2},{2,3},{3,4},{4,5},{5,6},{6,7},{7,8},{8,9},{9,10},{10,1... | collective-permute-start | bytes 1572872 | tf_op jit(solution)/shard_map/ppermute | solution.py:29
  314.7 4.4 copy-start.7
  314.7 4.4 copy-start.8
  316.5 37.5 %collective-permute-start.5 = (bf16[512,512]{1,0:T(8,128)(2,1)}, bf16[512,512]{1,0:T(8,128)(2,1)}, u32[]{:S(2)}, u32[]{:S(2)}) collective-permute-start(bf16[512,512]{1,0:T(8,128)(2,1)} %copy_bitcast_fusion.1), channel_id=1, source_target_pairs={{1,0},{2,1},{3,2},{4,3},{5,4},{6,5},{7,6},{8,7},{9,8},{10,9},{11,1... | collective-permute-start | bytes 1572872 | tf_op jit(solution)/shard_map/ppermute | solution.py:29
  317.8 34.6 %collective-permute-start.4 = (bf16[512,512]{1,0:T(8,128)(2,1)}, bf16[512,512]{1,0:T(8,128)(2,1)}, u32[]{:S(2)}, u32[]{:S(2)}) collective-permute-start(bf16[512,512]{1,0:T(8,128)(2,1)} %copy_bitcast_fusion.2), channel_id=1, source_target_pairs={{1,0},{2,1},{3,2},{4,3},{5,4},{6,5},{7,6},{8,7},{9,8},{10,9},{11,1... | collective-permute-start | bytes 1572872 | tf_op jit(solution)/shard_map/ppermute | solution.py:29
  322.8 2.9 copy-start.18
  328.3 6.8 %copy-start.4 = (bf16[512,4,128]{0,2,1:T(8,128)(2,1)S(1)}, bf16[512,4,128]{0,2,1:T(8,128)(2,1)}, u32[]{:S(2)}) copy-start(bf16[512,4,128]{0,2,1:T(8,128)(2,1)} %copy.68) | copy-start | bytes 1572868 | tf_op jit(solution)/shard_map/cond
  335.1 8.6 %copy-start.2 = (bf16[512,4,128]{2,1,0:T(4,128)(2,1)S(1)}, bf16[512,4,128]{2,1,0:T(4,128)(2,1)}, u32[]{:S(2)}) copy-start(bf16[512,4,128]{2,1,0:T(4,128)(2,1)} %get-tuple-element.349) | copy-start | bytes 1572868 | tf_op jit(solution)/shard_map/cond
  343.8 3.4 copy-start.1
  350.6 4.9 copy-start.9
  350.6 4.9 copy-start.10
  361.5 104.6 %copy-start.15 = (bf16[512,512]{1,0:T(8,128)(2,1)S(1)}, bf16[512,512]{1,0:T(8,128)(2,1)}, u32[]{:S(2)}) copy-start(bf16[512,512]{1,0:T(8,128)(2,1)} %param.22) | copy-start | bytes 1572868
  361.6 184.7 %all-reduce.7.cloned.1.call-start = ((), (), s32[]{:S(2)}) async-start(), calls=%async_computation.2 | async-start | bytes 163840 | tf_op jit(solution)/shard_map/psum | solution.py:285
  468.4 4.6 copy-start.13
  (5 other events, 8.9 us)
Sparse Core Ops, SparseCore 0:
  361.7 111.2 reduce-scatter.1
  475.3 70.9 all-reduce.6
where the time goes:
time: 559 us; the launch traced here: 555 us
  loops' own time  158 us (28%)
  blocking collectives  118 us (21%)
  local copies, waits for them, and re-layouts  81.7 us (15%)
  waiting for transfers between devices  71.1 us (13%)
  other arithmetic  51.5 us (9%)
  matrix products  42.1 us (8%)
  between operations  20.3 us (4%)
  starting transfers between devices  12.8 us (2%)
    another operation x1, loops' own time, entering(): return lax.fori_loop(0, count - 1, turn, total)  157 us
    psum x1, blocking collectives, body(): grad_mix = lax.psum(grad_mix, ('dp', 'seq'))  101 us
    psum x1, waiting for transfers between devices, body(): lax.psum(jnp.concatenate([proj_part, out_part], 1).astype(jnp.bfloat16),...  71 us
    dynamic_slice x62, local copies, waits for them, and re-layouts, turn(): longer = join(total, jax.tree.map(lambda part: part[position], pieces))  39.3 us
    eq x31, other arithmetic, combine(): joined = jnp.where((whole_b == 1) & same, total_a + total_b, total_b)  20.3 us
    unnamed x1, blocking collectives  16.6 us
    ppermute x6, starting transfers between devices, shifted(): return lax.ppermute(array, axis, pairs)  12.7 us
  transfers between devices with their start and end apart: 8, of which 1 were waited for; matrix products, arithmetic and copies ran while one was open for 27% of the time, Pallas kernels for 0%

commit v1 on v0

--- a/solution.py
+++ b/solution.py
@@ -7,6 +7,9 @@
 REACH = 1
 EPSILON = 1e-05
 HIGH = lax.Precision.HIGHEST
+guide_the_weights = lambda x_in, lane_axis, group_axis: lax.psum(
+    lax.psum(x_in, lane_axis), group_axis
+)
 
 
 def entering(value, axis, join, neutral):
@@ -287,7 +290,7 @@
     grad_mix = jnp.einsum(
         "ehf,ef->hf", grad_qtime[:, :, :freq_count], cosines, precision=HIGH
     ) + jnp.einsum("ehf,ef->hf", grad_qtime[:, :, freq_count:], sines, precision=HIGH)
-    grad_mix = lax.psum(grad_mix, ("dp", "seq"))
+    grad_mix = guide_the_weights(grad_mix, lane_axis="dp", group_axis="seq")
     factor = float(lax.axis_size("dp") * seq_devices * count) ** (-0.5)
     grad_proj = shard[:, : 4 * model_width] * factor
     grad_out_weight = shard[:, 4 * model_width :] * factor

time: 559 us -> 569 us (1.018)
  loops' own time: 158 us -> 165 us
    another operation x1, loops' own time: 157 us -> 165 us  [entering(): return lax.fori_loop(0, count - 1, turn, total)]
    psum x1 -> x2, blocking collectives: 101 us -> 100 us  [the longest x1 82.1 us: lax.psum(lax.psum(x_in, lane_axis), group_axis)]
  transfers between devices with their start and end apart: 8 -> 8, of which waited for: 1 -> 2; matrix products, arithmetic and copies ran while one was open for 27% -> 27% of each run, Pallas kernels for 0% -> 0%
where the time goes in v1:
time: 569 us; the launch traced here: 565 us
  loops' own time  165 us (29%)
  blocking collectives  117 us (21%)
  local copies, waits for them, and re-layouts  83.6 us (15%)
  waiting for transfers between devices  72.5 us (13%)
  other arithmetic  51.7 us (9%)
  matrix products  42.1 us (7%)
  between operations  20.4 us (4%)
  starting transfers between devices  12.8 us (2%)
    another operation x1, loops' own time, entering(): return lax.fori_loop(0, count - 1, turn, total)  165 us
    psum x1, blocking collectives, lax.psum(lax.psum(x_in, lane_axis), group_axis)  82.1 us
    psum x1, waiting for transfers between devices, body(): lax.psum(jnp.concatenate([proj_part, out_part], 1).astype(jnp.bfloat16),...  71.1 us
    dynamic_slice x62, local copies, waits for them, and re-layouts, turn(): longer = join(total, jax.tree.map(lambda part: part[position], pieces))  41.1 us
    eq x31, other arithmetic, combine(): joined = jnp.where((whole_b == 1) & same, total_a + total_b, total_b)  20.4 us
    psum x1, blocking collectives, lax.psum(x_in, lane_axis)  17.9 us
    unnamed x1, blocking collectives  16.6 us
    ppermute x6, starting transfers between devices, shifted(): return lax.ppermute(array, axis, pairs)  12.7 us
  transfers between devices with their start and end apart: 8, of which 2 were waited for; matrix products, arithmetic and copies ran while one was open for 27% of the time, Pallas kernels for 0%

profile of v1, /device:TPU:32, one launch (start us, length us, event | category | flops | bytes accessed | tf_op | source)
XLA Modules:
  0.0 564.6 jit_solution(4729112813480760907)
XLA Ops:
  16.5 3.6 gather_fusion.1
  20.1 3.5 gather_fusion
  27.8 16.6 %all-reduce.4 = (s32[32]{0:T(128)S(1)}, s32[32]{0:T(128)S(1)}, s32[32]{0:T(128)S(1)}, s32[32]{0:T(128)S(1)}) all-reduce(s32[32]{0:T(128)S(1)} %dynamic-update-slice, s32[32]{0:T(128)S(1)} %bitcast_dynamic-update-slice_fusion.1, s32[32]{0:T(128)S(1)} %bitcast_dynamic-update-slice_fusion, ...), channel_id=1, replica_groups=mesh['dp'=8,'seq'=32] {'seq'}, use_global_device_ids=true, to_apply=%add | all-reduce | flops 128 | bytes 1024
  44.4 226.1 %while.17 = (s32[]{:T(128)}, s32[1]{0:T(128)}, s32[1]{0:T(128)}, s32[1]{0:T(128)}, s32[]{:T(128)}, /*index=5*/s32[32,1]{0,1:T(1,128)S(1)}, s32[32,1]{0,1:T(1,128...) while((s32[]{:T(128)}, s32[1]{0:T(128)}, s32[1]{0:T(128)}, s32[1]{0:T(128)}, ...), condition=%wide.region_6.7_spmd, body=%wide.region_5.6_spmd.sunk | while | flops 18 | bytes 315 | solution.py:26
  274.8 3.6 multiply_convert_fusion
  280.9 3.8 collective-permute-start.3
  297.7 10.0 %conditional.5 = (f32[512,4,128]{2,0,1:T(8,128)}) conditional(s32[]{:T(128)} %bitcast.54, () %tuple.57, (bf16[512]{0:T(512)(128)(2,1)S(1)}, s32[512]{0:T(512)S(1)}, bf16[512,4,128]{2,1,0:T(4,128)(2,1)S(1)}, bf16[512,4,128]{2,1,0:T(4,128)(2,1)}, bf16[512,128]{1,0:T(8,128)(2,1)S(1)}, /*index=5*/bf16[512,4,128]{2,0,1:T(8,128)(2,1)S(1)}, ...), branch_computations={%region_9.10_spmd, %region_10.11_spmd} | conditional | flops 815268352 | bytes 12195848 | solution.py:229
  298.8 3.7 fusion.14
  302.5 5.2 fusion.12
  319.0 2.8 multiply_convert_fusion.1
  328.4 29.8 %conditional.6 = (f32[512,4,128]{2,0,1:T(8,128)}, f32[512,4,128]{2,0,1:T(8,128)}, f32[512,512]{1,0:T(8,128)}, f32[512,512]{1,0:T(8,128)}) conditional(s32[]{:T(128)} %bitcast.54, () %tuple.59, (bf16[512]{0:T(512)(128)(2,1)S(1)}, s32[512]{0:T(512)S(1)}, bf16[512,4,128]{2,1,0:T(4,128)(2,1)}, bf16[512,4,128]{2,1,0:T(4,128)(2,1)}, ...), branch_computations={%region_13.14_spmd, %region_14.15_spmd} | conditional | flops 1900020224 | bytes 65018056 | solution.py:253
  335.2 2.4 fusion.22
  337.6 4.3 select_convert_fusion.3
  341.9 2.5 copy.107
  344.4 3.5 fusion.23
  348.0 2.5 copy.53
  350.5 2.6 copy.109
  353.1 3.4 fusion.24
  374.0 17.9 %psum.22 = f32[4,64]{1,0:T(4,128)S(1)} all-reduce(f32[4,64]{1,0:T(4,128)S(1)} %add_bitcast_fusion.3), channel_id=1, replica_groups=mesh['dp'=8,'seq'=32] {'dp'}, use_global_device_ids=true, to_apply=%region_20.21 | all-reduce | flops 256 | bytes 2048 | tf_op jit(solution)/shard_map/psum | solution.py:11
  391.9 82.1 %psum.23 = f32[4,64]{1,0:T(4,128)S(1)} all-reduce(f32[4,64]{1,0:T(4,128)S(1)} %psum.22), channel_id=1, replica_groups=mesh['dp'=8,'seq'=32] {'seq'}, use_global_device_ids=true, to_apply=%region_21.22 | all-reduce | flops 256 | bytes 2048 | tf_op jit(solution)/shard_map/psum | solution.py:10
  474.0 2.3 fusion.54
  476.9 3.9 fusion.56
  482.2 2.3 fusion.67
  484.5 71.1 %all-reduce.7.cloned.1.call-done = bf16[16,2560]{1,0:T(8,128)(2,1)} async-done(((bf16[16,2560]{1,0:T(8,128)(2,1)}), bf16[16,2560]{1,0:T(8,128)(2,1)}) %all-reduce.7.cloned.1.call-update) | async-done | bytes 81936 | tf_op jit(solution)/shard_map/psum | solution.py:288
  (233 shorter events, 136.9 us)
Async XLA Ops:
  7.2 267.6 %copy-start = (bf16[512,2048]{1,0:T(8,128)(2,1)S(1)}, bf16[512,2048]{1,0:T(8,128)(2,1)}, u32[]{:S(2)}) copy-start(bf16[512,2048]{1,0:T(8,128)(2,1)} %param.21) | copy-start | bytes 6291460
  7.2 16.4 %copy-start.23 = (u32[256]{0:T(256)S(1)}, u32[256]{0:T(256)}, u32[]{:S(2)}) copy-start(u32[256]{0:T(256)} %constant.130) | copy-start | bytes 3076
  7.2 263.4 %copy-start.20 = (s32[1,512]{1,0:T(1,128)S(1)}, s32[1,512]{1,0:T(1,128)}, u32[]{:S(2)}) copy-start(s32[1,512]{1,0:T(1,128)} %param.19) | copy-start | bytes 6148
  7.2 263.4 %copy-start.22 = (f32[64]{0:T(128)S(1)}, f32[64]{0:T(128)}, u32[]{:S(2)}) copy-start(f32[64]{0:T(128)} %param.23) | copy-start | bytes 772
  7.2 267.3 %copy-start.5 = (bf16[1,512,512]{2,1,0:T(8,128)(2,1)S(1)}, bf16[1,512,512]{2,1,0:T(8,128)(2,1)}, u32[]{:S(2)}) copy-start(bf16[1,512,512]{2,1,0:T(8,128)(2,1)} %param.18) | copy-start | bytes 1572868
  7.2 474.9 %reduce-scatter.2.cloned.1.call-start = ((), (), s32[]{:S(2)}) async-start(), calls=%async_computation.1 | async-start | bytes 2703360 | tf_op jit(solution)/shard_map/reduce_scatter | solution.py:289
  8.1 299.6 %collective-permute-start = (bf16[512]{0:T(512)(128)(2,1)S(1)}, bf16[512]{0:T(512)(128)(2,1)}, u32[]{:S(2)}, u32[]{:S(2)}) collective-permute-start(bf16[512]{0:T(512)(128)(2,1)S(1)} %convert_reduce_fusion), channel_id=1, source_target_pairs={{0,1},{1,2},{2,3},{3,4},{4,5},{5,6},{6,7},{7,8},{8,9},{9,10},{10,1... | collective-permute-start | bytes 3080 | tf_op jit(solution)/shard_map/ppermute | solution.py:32
  272.6 41.6 %collective-permute-start.2 = (bf16[512,128]{1,0:T(8,128)(2,1)S(1)}, bf16[512,128]{1,0:T(8,128)(2,1)}, u32[]{:S(2)}, u32[]{:S(2)}) collective-permute-start(bf16[512,128]{1,0:T(8,128)(2,1)S(1)} %pad_maximum_fusion.2), channel_id=1, source_target_pairs={{0,1},{1,2},{2,3},{3,4},{4,5},{5,6},{6,7},{7,8},{8,9},{9,10},{10,1... | collective-permute-start | bytes 393224 | tf_op jit(solution)/shard_map/ppermute | solution.py:32
  274.8 12.1 %copy-start.21 = (f32[4,64]{1,0:T(4,128)S(1)}, f32[4,64]{1,0:T(4,128)}, u32[]{:S(2)}) copy-start(f32[4,64]{1,0:T(4,128)} %param.24) | copy-start | bytes 3076
  280.9 29.4 %collective-permute-start.3 = (bf16[512,512]{1,0:T(8,128)(2,1)}, bf16[512,512]{1,0:T(8,128)(2,1)}, u32[]{:S(2)}, u32[]{:S(2)}) collective-permute-start(bf16[512,512]{1,0:T(8,128)(2,1)} %get-tuple-element.395), channel_id=1, source_target_pairs={{0,1},{1,2},{2,3},{3,4},{4,5},{5,6},{6,7},{7,8},{8,9},{9,10},{10,1... | collective-permute-start | bytes 1572872 | tf_op jit(solution)/shard_map/ppermute | solution.py:32
  284.8 27.5 %collective-permute-start.1 = (bf16[512,512]{1,0:T(8,128)(2,1)}, bf16[512,512]{1,0:T(8,128)(2,1)}, u32[]{:S(2)}, u32[]{:S(2)}) collective-permute-start(bf16[512,512]{1,0:T(8,128)(2,1)} %get-tuple-element.396), channel_id=1, source_target_pairs={{0,1},{1,2},{2,3},{3,4},{4,5},{5,6},{6,7},{7,8},{8,9},{9,10},{10,1... | collective-permute-start | bytes 1572872 | tf_op jit(solution)/shard_map/ppermute | solution.py:32
  324.0 4.4 copy-start.7
  324.0 4.4 copy-start.8
  325.8 37.5 %collective-permute-start.5 = (bf16[512,512]{1,0:T(8,128)(2,1)}, bf16[512,512]{1,0:T(8,128)(2,1)}, u32[]{:S(2)}, u32[]{:S(2)}) collective-permute-start(bf16[512,512]{1,0:T(8,128)(2,1)} %copy_bitcast_fusion.1), channel_id=1, source_target_pairs={{1,0},{2,1},{3,2},{4,3},{5,4},{6,5},{7,6},{8,7},{9,8},{10,9},{11,1... | collective-permute-start | bytes 1572872 | tf_op jit(solution)/shard_map/ppermute | solution.py:32
  327.1 34.6 %collective-permute-start.4 = (bf16[512,512]{1,0:T(8,128)(2,1)}, bf16[512,512]{1,0:T(8,128)(2,1)}, u32[]{:S(2)}, u32[]{:S(2)}) collective-permute-start(bf16[512,512]{1,0:T(8,128)(2,1)} %copy_bitcast_fusion.2), channel_id=1, source_target_pairs={{1,0},{2,1},{3,2},{4,3},{5,4},{6,5},{7,6},{8,7},{9,8},{10,9},{11,1... | collective-permute-start | bytes 1572872 | tf_op jit(solution)/shard_map/ppermute | solution.py:32
  332.1 2.9 copy-start.18
  337.6 6.8 %copy-start.4 = (bf16[512,4,128]{0,2,1:T(8,128)(2,1)S(1)}, bf16[512,4,128]{0,2,1:T(8,128)(2,1)}, u32[]{:S(2)}) copy-start(bf16[512,4,128]{0,2,1:T(8,128)(2,1)} %copy.68) | copy-start | bytes 1572868 | tf_op jit(solution)/shard_map/cond
  344.4 8.6 %copy-start.2 = (bf16[512,4,128]{2,1,0:T(4,128)(2,1)S(1)}, bf16[512,4,128]{2,1,0:T(4,128)(2,1)}, u32[]{:S(2)}) copy-start(bf16[512,4,128]{2,1,0:T(4,128)(2,1)} %get-tuple-element.349) | copy-start | bytes 1572868 | tf_op jit(solution)/shard_map/cond
  353.1 3.4 copy-start.1
  359.9 4.9 copy-start.9
  359.9 4.9 copy-start.10
  370.9 103.2 %copy-start.15 = (bf16[512,512]{1,0:T(8,128)(2,1)S(1)}, bf16[512,512]{1,0:T(8,128)(2,1)}, u32[]{:S(2)}) copy-start(bf16[512,512]{1,0:T(8,128)(2,1)} %param.22) | copy-start | bytes 1572868
  370.9 184.7 %all-reduce.7.cloned.1.call-start = ((), (), s32[]{:S(2)}) async-start(), calls=%async_computation.2 | async-start | bytes 163840 | tf_op jit(solution)/shard_map/psum | solution.py:288
  476.3 5.9 %copy-start.13 = (bf16[1,512,512]{2,1,0:T(8,128)(2,1)S(1)}, bf16[1,512,512]{2,1,0:T(8,128)(2,1)}, u32[]{:S(2)}) copy-start(bf16[1,512,512]{2,1,0:T(8,128)(2,1)} %param.25) | copy-start | bytes 1572868
  (5 other events, 8.9 us)
Sparse Core Ops, SparseCore 0:
  371.0 111.0 reduce-scatter.1
  484.5 71.0 all-reduce.6
